TPU v7x, 32 devices: a whole 2x2x4 slice. The times are simulated.
32 devices in a mesh: row: 8 (over z, x), col: 4 (over y, core).
Axes of the slice: x: 2, y: 2, z: 4, core: 2. Of those that a mesh axis runs over, the one named last changes fastest.
Arguments:
- tokens: bfloat16 [4096, 768], P(('row', 'col')), may hold values from -6 to 6
- w_qkv: bfloat16 [768, 3, 768], P('row', None, 'col'), may hold values from -0.21875 to 0.21875
- w_out: bfloat16 [768, 768], P('col', 'row'), may hold values from -2.5 to 2.5
- w_gate_up: bfloat16 [768, 2, 3072], P('row', None, 'col'), may hold values from -0.21875 to 0.21875
- w_down: bfloat16 [3072, 768], P('col', 'row'), may hold values from -0.109375 to 0.109375
- gain1: float32 [768], replicated, may hold values from 0.1 to 1.9
- bias1: float32 [768], replicated, may hold values from -1.8 to 1.8
- gain2: float32 [768], replicated, may hold values from 0.1 to 1.9
- bias2: float32 [768], replicated, may hold values from -1.8 to 1.8
- cotangent: bfloat16 [4096, 768], P(('row', 'col')), may hold values from -6 to 6
- seq_lengths: int32 [3], replicated, may hold values from 512 to 2048, as said below
- packed_order: int32 [4096], replicated, may hold values from 0 to 4095, each once
Outputs:
- output: bfloat16 [4096, 768], P(('row', 'col'))
- grad_tokens: float32 [4096, 768], P(('row', 'col'))
- grad_w_qkv: float32 [768, 3, 768], P('row', None, 'col')
- grad_w_out: float32 [768, 768], P('col', 'row')
- grad_w_gate_up: float32 [768, 2, 3072], P('row', None, 'col')
- grad_w_down: float32 [3072, 768], P('col', 'row')
- grad_gain1: float32 [768], replicated
- grad_bias1: float32 [768], replicated
- grad_gain2: float32 [768], replicated
- grad_bias2: float32 [768], replicated
Inputs may be any that keep to these rules, and one draw needn't show every extreme that they name: `seq_lengths`: 3 lengths that sum to 4096; the longest is exactly 2048.
All inputs are finite; a program needn't handle non-finite values.
Results may differ from a plain program's by a relative error of at most 0.024.
Values may be sent and summed in bfloat16 or wider, within the bound.
No kernel may reach another device: no remote copies, remote signals or barrier semaphores. Data moves between devices by JAX's collectives and lax.ppermute only.
A program may use at most 512 MiB of HBM per device.

v0:
```python
import math
import jax
import jax.numpy as jnp
from jax import lax
from jax.sharding import PartitionSpec as P

HEAD = 64
ROPE_BASE = 1000.0
NORM_EPS = 1e-12
MASKED = -1e30


def token_layout(seq_lengths, packed_order):
    seq_ends = jnp.cumsum(seq_lengths)
    seq_starts = seq_ends - seq_lengths
    seq_id = jnp.sum((packed_order[:, None] >= seq_ends[None, :]).astype(jnp.int32), axis=1)
    member = seq_id[:, None] == jnp.arange(seq_lengths.shape[0], dtype=jnp.int32)[None, :]
    start_of = jnp.sum(jnp.where(member, seq_starts[None, :], 0), axis=1)
    return (seq_id, packed_order - start_of)


def rope_tables(positions, head):
    half = head // 2
    freqs = ROPE_BASE ** (-jnp.arange(half, dtype=jnp.float32) * 2.0 / head)
    angles = positions.astype(jnp.float32)[:, None] * freqs[None, :]
    return (jnp.cos(angles), jnp.sin(angles))


def rotate(field, cosine, sine):
    half = field.shape[-1] // 2
    first = field[..., :half]
    second = field[..., half:]
    cos_b = cosine[:, None, :]
    sin_b = sine[:, None, :]
    return jnp.concatenate(
        [first * cos_b - second * sin_b, second * cos_b + first * sin_b], axis=-1
    )


def rotate_back(field, cosine, sine):
    half = field.shape[-1] // 2
    first = field[..., :half]
    second = field[..., half:]
    cos_b = cosine[:, None, :]
    sin_b = sine[:, None, :]
    return jnp.concatenate(
        [first * cos_b + second * sin_b, second * cos_b - first * sin_b], axis=-1
    )


def norm_forward(values, gain, bias):
    centered = values - jnp.mean(values, axis=-1, keepdims=True)
    inverse = lax.rsqrt(jnp.mean(centered * centered, axis=-1, keepdims=True) + NORM_EPS)
    normed = centered * inverse
    return (normed * gain + bias, normed, inverse)


def norm_backward(grad_out, normed, inverse, gain):
    scaled = grad_out * gain
    grad_in = inverse * (
        scaled
        - jnp.mean(scaled, axis=-1, keepdims=True)
        - normed * jnp.mean(scaled * normed, axis=-1, keepdims=True)
    )
    return (grad_in, jnp.sum(grad_out * normed, axis=0), jnp.sum(grad_out, axis=0))


def gather_rows(rows):
    return lax.all_gather(rows, "col", axis=0, tiled=True)


def gather_grads(rows):
    return lax.all_gather(rows, "col", axis=0, tiled=True)


def column_sum(left, product):
    return lax.psum_scatter(
        product(left).astype(jnp.bfloat16), "col", scatter_dimension=0, tiled=True
    ).astype(jnp.float32)


def score_block(queries, seg_queries, key_rows, seg_keys, scale):
    count = key_rows.shape[0]
    heads = queries.shape[1]
    head = queries.shape[2]
    scores = (
        jnp.einsum(
            "qhd,khd->hqk",
            queries,
            key_rows.reshape(count, heads, head),
            preferred_element_type=jnp.float32,
        )
        * scale
    )
    same = seg_queries[:, None] == seg_keys[None, :]
    return (scores, same)


def probabilities(queries, seg_queries, log_total, key_rows, seg_keys, scale):
    scores, same = score_block(queries, seg_queries, key_rows, seg_keys, scale)
    return jnp.where(same[None], jnp.exp(scores - log_total[..., None]), 0.0)


def score_grads(probs, grad_heads, delta, value_rows):
    count = value_rows.shape[0]
    heads = grad_heads.shape[1]
    head = grad_heads.shape[2]
    grad_probs = jnp.einsum(
        "qhd,khd->hqk",
        grad_heads,
        value_rows.reshape(count, heads, head),
        preferred_element_type=jnp.float32,
    )
    return (probs * (grad_probs - delta[..., None])).astype(jnp.bfloat16)


def local(
    tokens,
    w_qkv,
    w_out,
    w_gate_up,
    w_down,
    gain1,
    bias1,
    gain2,
    bias2,
    cotangent,
    seq_lengths,
    packed_order,
):
    row_index = lax.axis_index("row")
    shards = lax.axis_size("row")
    full_qkv, full_out, full_gate_up, full_down = (
        lax.all_gather(w_qkv, "row", axis=0, tiled=True),
        lax.all_gather(w_out, "row", axis=1, tiled=True),
        lax.all_gather(w_gate_up, "row", axis=0, tiled=True),
        lax.all_gather(w_down, "row", axis=1, tiled=True),
    )
    seq_all, positions = token_layout(seq_lengths, packed_order)
    token_block = gather_rows(tokens)
    group = token_block.shape[0]
    first_slot = row_index * group
    seg_rows = lax.dynamic_slice_in_dim(seq_all, first_slot, group, 0)
    cosine, sine = rope_tables(lax.dynamic_slice_in_dim(positions, first_slot, group, 0), HEAD)
    width = full_qkv.shape[2]
    local_heads = width // HEAD
    scale = 1.0 / math.sqrt(HEAD)
    mixed = jnp.einsum("td,dce->tce", token_block, full_qkv, preferred_element_type=jnp.float32)
    query_bf = rotate(mixed[:, 0].reshape(group, local_heads, HEAD), cosine, sine).astype(
        jnp.bfloat16
    )
    key_bf = (
        rotate(mixed[:, 1].reshape(group, local_heads, HEAD), cosine, sine)
        .astype(jnp.bfloat16)
        .reshape(group, width)
    )
    value_bf = mixed[:, 2].astype(jnp.bfloat16)
    run_max = jnp.full((local_heads, group), MASKED, jnp.float32)
    key_piece = lax.all_gather(key_bf, "row", axis=0, tiled=True)
    value_piece = lax.all_gather(value_bf, "row", axis=0, tiled=True)
    count = key_piece.shape[0]
    seg_keys = seq_all
    scores, same = score_block(query_bf, seg_rows, key_piece, seg_keys, scale)
    new_max = jnp.maximum(run_max, jnp.max(jnp.where(same[None], scores, MASKED), axis=-1))
    weights_now = jnp.where(same[None], jnp.exp(scores - new_max[..., None]), 0.0)
    new_total = jnp.sum(weights_now, axis=-1)
    new_acc = jnp.einsum(
        "hqk,khd->hqd",
        weights_now.astype(jnp.bfloat16),
        value_piece.reshape(count, local_heads, HEAD),
        preferred_element_type=jnp.float32,
    )
    context = new_acc / new_total[..., None]
    log_total = new_max + jnp.log(new_total)
    context_bf = jnp.transpose(context, (1, 0, 2)).reshape(group, width).astype(jnp.bfloat16)

    def out_product(rows):
        return jnp.dot(rows, full_out, preferred_element_type=jnp.float32)

    attn_out = column_sum(context_bf, out_product)
    residual1 = tokens.astype(jnp.float32) + attn_out
    hidden1, normed1, inverse1 = norm_forward(residual1, gain1, bias1)
    hidden_block = gather_rows(hidden1.astype(jnp.bfloat16))
    gate_up = jnp.einsum(
        "td,dcf->tcf", hidden_block, full_gate_up, preferred_element_type=jnp.float32
    )
    up = gate_up[:, 0]
    gate = gate_up[:, 1]
    sigma = jax.nn.sigmoid(gate)
    inner = (gate * sigma * up).astype(jnp.bfloat16)

    def down_product(rows):
        return jnp.dot(rows, full_down, preferred_element_type=jnp.float32)

    ffn_out = column_sum(inner, down_product)
    residual2 = hidden1 + ffn_out
    result, normed2, inverse2 = norm_forward(residual2, gain2, bias2)
    grad_res2, grad_gain2, grad_bias2 = norm_backward(
        cotangent.astype(jnp.float32), normed2, inverse2, gain2
    )
    grad_ffn = gather_grads(grad_res2.astype(jnp.bfloat16))
    grad_inner = lax.dot_general(
        grad_ffn, full_down, (((1,), (1,)), ((), ())), preferred_element_type=jnp.float32
    )
    grad_down = lax.dot_general(
        inner, grad_ffn, (((0,), (0,)), ((), ())), preferred_element_type=jnp.float32
    )
    grad_up = grad_inner * gate * sigma
    grad_gate = grad_inner * up * sigma * (1.0 + gate * (1.0 - sigma))
    grad_gate_up = jnp.stack([grad_up, grad_gate], axis=1).astype(jnp.bfloat16)

    def gate_up_back(rows):
        return jnp.einsum("tcf,dcf->td", rows, full_gate_up, preferred_element_type=jnp.float32)

    grad_hidden1 = grad_res2 + column_sum(grad_gate_up, gate_up_back)
    grad_wgu = jnp.einsum(
        "td,tcf->dcf", hidden_block, grad_gate_up, preferred_element_type=jnp.float32
    )
    grad_res1, grad_gain1, grad_bias1 = norm_backward(grad_hidden1, normed1, inverse1, gain1)
    grad_attn = gather_grads(grad_res1.astype(jnp.bfloat16))
    grad_wo = lax.dot_general(
        context_bf, grad_attn, (((0,), (0,)), ((), ())), preferred_element_type=jnp.float32
    )
    grad_context_bf = lax.dot_general(
        grad_attn, full_out, (((1,), (1,)), ((), ())), preferred_element_type=jnp.float32
    ).astype(jnp.bfloat16)
    grad_heads = grad_context_bf.reshape(group, local_heads, HEAD)
    delta = jnp.sum(jnp.transpose(grad_heads, (1, 0, 2)).astype(jnp.float32) * context, axis=-1)
    key_all, value_all = (
        lax.all_gather(key_bf, "row", axis=0, tiled=True),
        lax.all_gather(value_bf, "row", axis=0, tiled=True),
    )
    tokens_total = key_all.shape[0]
    per_turn = group * math.gcd(shards, max(1, 2048 // group))
    turns = tokens_total // per_turn

    def turn_terms(turn):
        begin = turn * per_turn
        key_rows = lax.dynamic_slice_in_dim(key_all, begin, per_turn, 0)
        value_rows = lax.dynamic_slice_in_dim(value_all, begin, per_turn, 0)
        seg_keys = lax.dynamic_slice_in_dim(seq_all, begin, per_turn, 0)
        probs = probabilities(query_bf, seg_rows, log_total, key_rows, seg_keys, scale)
        grad_scores = score_grads(probs, grad_heads, delta, value_rows)
        return (begin, key_rows, probs, grad_scores)

    def query_term(grad_scores, key_rows):
        return jnp.einsum(
            "hqk,khd->qhd",
            grad_scores,
            key_rows.reshape(per_turn, local_heads, HEAD),
            preferred_element_type=jnp.float32,
        )

    empty_query = jnp.zeros((group, local_heads, HEAD), jnp.float32)

    def key_turn(turn, carry):
        grad_query, grad_keys, grad_values = carry
        begin, key_rows, probs, grad_scores = turn_terms(turn)
        grad_query = grad_query + query_term(grad_scores, key_rows)
        key_term = jnp.einsum(
            "hqk,qhd->khd", grad_scores, query_bf, preferred_element_type=jnp.float32
        ).reshape(per_turn, width)
        value_term = jnp.einsum(
            "hqk,qhd->khd",
            probs.astype(jnp.bfloat16),
            grad_heads,
            preferred_element_type=jnp.float32,
        ).reshape(per_turn, width)
        grad_keys = lax.dynamic_update_slice_in_dim(grad_keys, key_term, begin, 0)
        grad_values = lax.dynamic_update_slice_in_dim(grad_values, value_term, begin, 0)
        return (grad_query, grad_keys, grad_values)

    empty_keys = jnp.zeros((tokens_total, width), jnp.float32)
    grad_query, grad_keys_all, grad_values_all = lax.fori_loop(
        0, turns, key_turn, (empty_query, empty_keys, empty_keys)
    )
    grad_key_rows, grad_value_rows = (
        lax.psum_scatter(grad_keys_all, "row", scatter_dimension=0, tiled=True),
        lax.psum_scatter(grad_values_all, "row", scatter_dimension=0, tiled=True),
    )
    grad_query_raw = rotate_back(grad_query * scale, cosine, sine).reshape(group, width)
    grad_key_raw = rotate_back(
        grad_key_rows.reshape(group, local_heads, HEAD) * scale, cosine, sine
    ).reshape(group, width)
    grad_mixed = jnp.stack([grad_query_raw, grad_key_raw, grad_value_rows], axis=1).astype(
        jnp.bfloat16
    )

    def qkv_back(rows):
        return jnp.einsum("tce,dce->td", rows, full_qkv, preferred_element_type=jnp.float32)

    grad_tokens = grad_res1 + column_sum(grad_mixed, qkv_back)
    grad_wqkv = jnp.einsum(
        "td,tce->dce", token_block, grad_mixed, preferred_element_type=jnp.float32
    )
    grad_w_qkv, grad_w_out, grad_w_gate_up, grad_w_down = (
        lax.psum_scatter(grad_wqkv, "row", scatter_dimension=0, tiled=True),
        lax.psum_scatter(grad_wo, "row", scatter_dimension=1, tiled=True),
        lax.psum_scatter(grad_wgu, "row", scatter_dimension=0, tiled=True),
        lax.psum_scatter(grad_down, "row", scatter_dimension=1, tiled=True),
    )
    norm_gain1, norm_bias1, norm_gain2, norm_bias2 = lax.psum(
        (grad_gain1, grad_bias1, grad_gain2, grad_bias2), ("row", "col")
    )
    return (
        result.astype(jnp.bfloat16),
        grad_tokens,
        grad_w_qkv,
        grad_w_out,
        grad_w_gate_up,
        grad_w_down,
        norm_gain1,
        norm_bias1,
        norm_gain2,
        norm_bias2,
    )


def solution(mesh):
    placed = (
        P(("row", "col"), None),
        P("row", None, "col"),
        P("col", "row"),
        P("row", None, "col"),
        P("col", "row"),
        P(),
        P(),
        P(),
        P(),
        P(("row", "col"), None),
        P(),
        P(),
    )
    return jax.shard_map(
        local,
        mesh=mesh,
        in_specs=placed,
        out_specs=(
            P(("row", "col"), None),
            P(("row", "col"), None),
            P("row", None, "col"),
            P("col", "row"),
            P("row", None, "col"),
            P("col", "row"),
            P(),
            P(),
            P(),
            P(),
        ),
        check_vma=False,
    )
```

profile of v0, /device:TPU:0, one launch (start us, length us, event | category | flops | bytes accessed | tf_op | source)
XLA Modules:
  0.0 918.4 jit_solution(15256059629411682818)
XLA Ops:
  9.8 38.8 %all_gather.33 = bf16[768,3,192]{2,1,0:T(4,128)(2,1)S(1)} all-gather(bf16[96,3,192]{2,1,0:T(4,128)(2,1)S(1)} %copy.45), channel_id=1, replica_groups=mesh['row'=8,'col'=4] {'row'}, dimensions={0}, use_global_device_ids=true | all-gather | bytes 995328 | tf_op jit(solution)/shard_map/all_gather | solution.py:134
  49.5 8.8 all_gather.32
  64.3 31.8 %all_gather.36 = bf16[192,768]{0,1:T(8,128)(2,1)S(1)} all-gather(bf16[192,96]{0,1:T(8,128)(2,1)S(1)} %copy.47), channel_id=1, replica_groups=mesh['row'=8,'col'=4] {'row'}, dimensions={1}, use_global_device_ids=true | all-gather | bytes 331776 | tf_op jit(solution)/shard_map/all_gather | solution.py:135
  96.1 11.8 %all-gather.6.cloned.1.call-done = bf16[4096,192]{0,1:T(8,128)(2,1)} async-done(((bf16[512,192]{0,1:T(8,128)(2,1)}), bf16[4096,192]{0,1:T(8,128)(2,1)}) %all-gather.6.cloned.1.call-update) | async-done | bytes 1572880 | tf_op jit(solution)/shard_map/all_gather | solution.py:159
  107.9 12.5 %select_reduce_fusion = (f32[3,512]{1,0:T(4,128)S(1)}, f32[3,512,4096]{2,1,0:T(8,128)}) fusion(pred[512,4096]{1,0:T(8,128)(4,1)S(1)} %broadcast_compare_fusion.1, bf16[4096,3,64]{0,2,1:T(8,128)(2,1)} %bitcast.162, bf16[512,3,32]{0,2,1:T(8,128)(2,1)S(1)} %get-tuple-element.336, bf16[512,3,32]{0,2,1:T(8,128)(2,1)S(1)} %get-tuple-element.335), kind=kOutput, calls=%fused_computation.16 | convolution fusion | flops 824572416 | bytes 29038592 | tf_op jit(solution)/shard_map/qhd,khd->hqk/dot_general | solution.py:87
  120.4 12.0 %fusion.8 = f32[3,512]{1,0:T(4,128)S(1)} fusion(f32[3,512,4096]{2,1,0:T(8,128)} %get-tuple-element.347, f32[3,512]{1,0:T(4,128)S(1)} %broadcast_maximum_fusion, pred[512,4096]{1,0:T(8,128)(4,1)S(1)} %broadcast_compare_fusion.1), kind=kLoop, calls=%fused_computation.17 | loop fusion | flops 25164288 | bytes 27275264 | tf_op jit(solution)/shard_map/reduce_sum | solution.py:166
  132.4 21.2 %all-gather.12.cloned.1.call-done = bf16[4096,1,192]{0,2,1:T(8,128)(2,1)} async-done(((bf16[512,1,192]{0,2,1:T(8,128)(2,1)}), bf16[4096,1,192]{0,2,1:T(8,128)(2,1)}) %all-gather.12.cloned.1.call-update) | async-done | bytes 1572880 | tf_op jit(solution)/shard_map/all_gather | solution.py:160
  153.6 12.0 %fusion.29 = (bf16[512,3,64]{0,2,1:T(8,128)(2,1)S(1)}, f32[3,512,64]{1,2,0:T(8,128)}) fusion(f32[512,3]{0,1:T(4,128)S(1)} %bitcast.183, bf16[4096,3,64]{0,2,1:T(8,128)(2,1)} %bitcast.163, f32[3,512,4096]{2,1,0:T(8,128)} %get-tuple-element.347, f32[3,512]{1,0:T(4,128)S(1)} %broadcast_maximum_fusion, pred[512,4096]{1,0:T(8,128)(4,1)S(1)} %broadcast_compare_fusion.1), kind=kOutput, calls=%fused_computation.58 | convolution fusion | flops 830668800 | bytes 29437952 | tf_op jit(solution)/shard_map/hqk,khd->hqd/dot_general | solution.py:167
  169.4 19.2 %reduce-scatter.15.cloned.1.call-done = bf16[128,768]{1,0:T(8,128)(2,1)} async-done(((bf16[512,768]{1,0:T(8,128)(2,1)}), bf16[128,768]{1,0:T(8,128)(2,1)}) %reduce-scatter.15.cloned.1.call-update) | async-done | bytes 196624 | tf_op jit(solution)/shard_map/reduce_scatter | solution.py:77
  191.8 8.4 all_gather.37
  200.2 43.2 %all-gather.8.cloned.1.call-done = bf16[768,2,768]{2,0,1:T(8,128)(2,1)} async-done(((bf16[96,2,768]{2,0,1:T(8,128)(2,1)}), bf16[768,2,768]{2,0,1:T(8,128)(2,1)}) %all-gather.8.cloned.1.call-update) | async-done | bytes 2359312 | tf_op jit(solution)/shard_map/all_gather | solution.py:136
  248.6 36.7 %all-gather.10.cloned.1.call-done = bf16[768,768]{0,1:T(8,128)(2,1)} async-done(((bf16[768,96]{0,1:T(8,128)(2,1)}), bf16[768,768]{0,1:T(8,128)(2,1)}) %all-gather.10.cloned.1.call-update) | async-done | bytes 1179664 | tf_op jit(solution)/shard_map/all_gather | solution.py:137
  288.3 22.1 %reduce-scatter.17.cloned.1.call-done = bf16[128,768]{1,0:T(8,128)(2,1)} async-done(((bf16[512,768]{1,0:T(8,128)(2,1)}), bf16[128,768]{1,0:T(8,128)(2,1)}) %reduce-scatter.17.cloned.1.call-update) | async-done | bytes 196624 | tf_op jit(solution)/shard_map/reduce_scatter | solution.py:77
  313.7 8.2 all_gather.40
  328.2 23.7 %reduce-scatter.19.cloned.1.call-done = bf16[128,768]{1,0:T(8,128)(2,1)} async-done(((bf16[512,768]{1,0:T(8,128)(2,1)}), bf16[128,768]{1,0:T(8,128)(2,1)}) %reduce-scatter.19.cloned.1.call-update) | async-done | bytes 196624 | tf_op jit(solution)/shard_map/reduce_scatter | solution.py:77
  368.2 58.9 %while.18 = (s32[]{:T(128)}, f32[512,3,64]{0,2,1:T(8,128)S(1)}, f32[4096,192]{0,1:T(8,128)}, f32[4096,192]{0,1:T(8,128)}, bf16[4096,192]{0,1:T(8,128)(2,1)S(1)},...) while((s32[]{:T(128)}, f32[512,3,64]{0,2,1:T(8,128)S(1)}, ...), condition=%wide.region_18.19_spmd.clone, body=%wide.region_17.18_spmd.clone.sunk | while | flops 2045968384 | bytes 107786520 | solution.py:274
  434.6 68.0 %reduce-scatter.21.cloned.1.call-done = f32[512,192]{0,1:T(8,128)} async-done(((f32[4096,192]{0,1:T(8,128)}), f32[512,192]{0,1:T(8,128)}) %reduce-scatter.21.cloned.1.call-update) | async-done | bytes 393232 | tf_op jit(solution)/shard_map/reduce_scatter | solution.py:278
  503.8 76.9 %reduce-scatter.23.cloned.1.call-done = f32[512,192]{0,1:T(8,128)} async-done(((f32[4096,192]{0,1:T(8,128)}), f32[512,192]{0,1:T(8,128)}) %reduce-scatter.23.cloned.1.call-update) | async-done | bytes 393232 | tf_op jit(solution)/shard_map/reduce_scatter | solution.py:279
  590.5 40.1 %all-reduce = (f32[768]{0:T(1024)}, f32[768]{0:T(1024)}, f32[768]{0:T(1024)}, f32[768]{0:T(1024)}) all-reduce(f32[768]{0:T(1024)S(1)} %get-tuple-element.283, f32[768]{0:T(1024)S(1)} %get-tuple-element.288, f32[768]{0:T(1024)S(1)} %copy-done.34, f32[768]{0:T(1024)S(1)} %copy-done.35), channel_id=1, replica_groups=mesh['row'=8,'col'=4] {'row','col'}, use_global_device_ids=true, to_apply=%region_27.28 | all-reduce | flops 3072 | bytes 24576 | tf_op jit(solution)/shard_map/psum | solution.py:302
  630.6 15.3 %reduce-scatter.33.cloned.1.call-done = f32[96,192]{1,0:T(8,128)} async-done(((f32[768,192]{1,0:T(8,128)}), f32[96,192]{1,0:T(8,128)}) %reduce-scatter.33.cloned.1.call-update) | async-done | bytes 73744
  647.6 96.2 %reduce-scatter.27.cloned.1.call-done = f32[96,2,768]{2,0,1:T(8,128)} async-done(((f32[768,2,768]{2,0,1:T(8,128)}), f32[96,2,768]{2,0,1:T(8,128)}) %reduce-scatter.27.cloned.1.call-update) | async-done | bytes 589840 | tf_op jit(solution)/shard_map/reduce_scatter | solution.py:299
  746.1 23.1 %reduce-scatter.25.cloned.1.call-done = bf16[128,768]{1,0:T(8,128)(2,1)} async-done(((bf16[512,768]{1,0:T(8,128)(2,1)}), bf16[128,768]{1,0:T(8,128)(2,1)}) %reduce-scatter.25.cloned.1.call-update) | async-done | bytes 196624 | tf_op jit(solution)/shard_map/reduce_scatter | solution.py:77
  771.0 69.1 %reduce-scatter.31.cloned.1.call-done = f32[96,576]{1,0:T(8,128)} async-done(((f32[768,576]{1,0:T(8,128)}), f32[96,576]{1,0:T(8,128)}) %reduce-scatter.31.cloned.1.call-update) | async-done | bytes 221200
  842.0 69.8 %reduce-scatter.29.cloned.1.call-done = f32[768,96]{0,1:T(8,128)} async-done(((f32[768,768]{0,1:T(8,128)}), f32[768,96]{0,1:T(8,128)}) %reduce-scatter.29.cloned.1.call-update) | async-done | bytes 294928 | tf_op jit(solution)/shard_map/reduce_scatter | solution.py:300
  (200 shorter events, 134.8 us)
Async XLA Ops:
  7.2 100.7 %all-gather.6.cloned.1.call-start = ((), (), s32[]{:S(2)}) async-start(), calls=%async_computation.10 | async-start | bytes 1769472 | tf_op jit(solution)/shard_map/all_gather | solution.py:159
  62.0 91.6 %all-gather.12.cloned.1.call-start = ((), (), s32[]{:S(2)}) async-start(), calls=%async_computation.21 | async-start | bytes 1769472 | tf_op jit(solution)/shard_map/all_gather | solution.py:160
  62.7 125.8 %reduce-scatter.15.cloned.1.call-start = ((), (), s32[]{:S(2)}) async-start(), calls=%async_computation.11 | async-start | bytes 983040 | tf_op jit(solution)/shard_map/reduce_scatter | solution.py:77
  167.0 76.4 %all-gather.8.cloned.1.call-start = ((), (), s32[]{:S(2)}) async-start(), calls=%async_computation.12 | async-start | bytes 2654208 | tf_op jit(solution)/shard_map/all_gather | solution.py:136
  168.8 116.5 %all-gather.10.cloned.1.call-start = ((), (), s32[]{:S(2)}) async-start(), calls=%async_computation.13 | async-start | bytes 1327104 | tf_op jit(solution)/shard_map/all_gather | solution.py:137
  169.3 141.1 %reduce-scatter.17.cloned.1.call-start = ((), (), s32[]{:S(2)}) async-start(), calls=%async_computation.14 | async-start | bytes 983040 | tf_op jit(solution)/shard_map/reduce_scatter | solution.py:77
  248.6 64.2 %copy-start.7 = (bf16[512,768]{1,0:T(8,128)(2,1)}, bf16[512,768]{1,0:T(8,128)(2,1)S(1)}, u32[]{:S(2)}) copy-start(bf16[512,768]{1,0:T(8,128)(2,1)S(1)} %multiply_convert_fusion.2) | copy-start | bytes 2359300
  248.6 63.4 %copy-start.20 = (bf16[128,768]{1,0:T(8,128)(2,1)S(1)}, bf16[128,768]{1,0:T(8,128)(2,1)}, u32[]{:S(2)}) copy-start(bf16[128,768]{1,0:T(8,128)(2,1)} %param.23) | copy-start | bytes 589828
  248.6 64.2 %copy-start.36 = (f32[768]{0:T(1024)S(1)}, f32[768]{0:T(1024)}, u32[]{:S(2)}) copy-start(f32[768]{0:T(1024)} %param.22) | copy-start | bytes 9220
  288.3 63.7 %reduce-scatter.19.cloned.1.call-start = ((), (), s32[]{:S(2)}) async-start(), calls=%async_computation.15 | async-start | bytes 983040 | tf_op jit(solution)/shard_map/reduce_scatter | solution.py:77
  328.1 174.4 %reduce-scatter.21.cloned.1.call-start = ((), (), s32[]{:S(2)}) async-start(), calls=%async_computation.16 | async-start | bytes 3538944 | tf_op jit(solution)/shard_map/reduce_scatter | solution.py:278
  427.2 153.5 %reduce-scatter.23.cloned.1.call-start = ((), (), s32[]{:S(2)}) async-start(), calls=%async_computation.17 | async-start | bytes 3538944 | tf_op jit(solution)/shard_map/reduce_scatter | solution.py:279
  427.9 218.0 %reduce-scatter.33.cloned.1.call-start = ((), (), s32[]{:S(2)}) async-start(), calls=%async_computation.23 | async-start | bytes 884736
  429.7 314.1 %reduce-scatter.27.cloned.1.call-start = ((), (), s32[]{:S(2)}) async-start(), calls=%async_computation.19 | async-start | bytes 5308416 | tf_op jit(solution)/shard_map/reduce_scatter | solution.py:299
  434.5 69.1 %copy-start.22 = (f32[512,32]{0,1:T(8,128)S(1)}, f32[512,32]{0,1:T(8,128)}, u32[]{:S(2)}) copy-start(f32[512,32]{0,1:T(8,128)} %copy-done.21) | copy-start | bytes 196612
  434.5 69.1 %copy-start.24 = (f32[512,32]{0,1:T(8,128)S(1)}, f32[512,32]{0,1:T(8,128)}, u32[]{:S(2)}) copy-start(f32[512,32]{0,1:T(8,128)} %copy-done.23) | copy-start | bytes 196612
  434.5 147.9 %copy-start.10 = (bf16[768,3,192]{0,2,1:T(8,128)(2,1)S(1)}, bf16[768,3,192]{0,2,1:T(8,128)(2,1)}, u32[]{:S(2)}) copy-start(bf16[768,3,192]{0,2,1:T(8,128)(2,1)} %copy-done.9) | copy-start | bytes 2654212
  434.5 334.8 %reduce-scatter.25.cloned.1.call-start = ((), (), s32[]{:S(2)}) async-start(), calls=%async_computation.18 | async-start | bytes 983040 | tf_op jit(solution)/shard_map/reduce_scatter | solution.py:77
  503.7 80.4 %copy-start.26 = (bf16[512,3,64]{0,2,1:T(8,128)(2,1)}, bf16[512,3,64]{0,2,1:T(8,128)(2,1)S(1)}, u32[]{:S(2)}) copy-start(bf16[512,3,64]{0,2,1:T(8,128)(2,1)S(1)} %pad_maximum_fusion.8) | copy-start | bytes 589828
  503.8 80.7 %copy-start.14 = (bf16[512,768]{1,0:T(8,128)(2,1)S(1)}, bf16[512,768]{1,0:T(8,128)(2,1)}, u32[]{:S(2)}) copy-start(bf16[512,768]{1,0:T(8,128)(2,1)} %copy-done.13) | copy-start | bytes 2359300
  503.8 80.4 %copy-start.27 = (bf16[512,3,64]{0,2,1:T(8,128)(2,1)}, bf16[512,3,64]{0,2,1:T(8,128)(2,1)S(1)}, u32[]{:S(2)}) copy-start(bf16[512,3,64]{0,2,1:T(8,128)(2,1)S(1)} %pad_maximum_fusion.9) | copy-start | bytes 589828
  584.2 255.8 %reduce-scatter.31.cloned.1.call-start = ((), (), s32[]{:S(2)}) async-start(), calls=%async_computation.22 | async-start | bytes 2211840
  588.1 323.7 %reduce-scatter.29.cloned.1.call-start = ((), (), s32[]{:S(2)}) async-start(), calls=%async_computation.20 | async-start | bytes 2654208 | tf_op jit(solution)/shard_map/reduce_scatter | solution.py:300
  590.5 178.8 %copy-start.17 = (f32[128,768]{1,0:T(8,128)S(1)}, f32[128,768]{1,0:T(8,128)}, u32[]{:S(2)}) copy-start(f32[128,768]{1,0:T(8,128)} %get-tuple-element.320) | copy-start | bytes 1179652
  (33 other events, 386.7 us)
Sparse Core Ops, SparseCore 0:
  62.1 45.7 all-gather.5
  110.5 43.0 all-gather.11
  167.1 21.4 reduce-scatter.14
  191.4 51.9 all-gather.7
  245.7 39.5 all-gather.9
  288.4 22.0 reduce-scatter.16
  328.3 23.6 reduce-scatter.18
  427.3 75.2 reduce-scatter.20
  506.6 74.0 reduce-scatter.22
  584.2 61.6 reduce-scatter.32
  649.6 94.1 reduce-scatter.26
  746.2 23.0 reduce-scatter.24
  773.1 66.8 reduce-scatter.30
  843.9 67.8 reduce-scatter.28
where the time goes:
time: 919 us; the launch traced here: 918 us
  waiting for transfers between devices  598 us (65%)
  blocking collectives  144 us (16%)
  matrix products  101 us (11%)
  other arithmetic  31.8 us (3%)
  local copies, waits for them, and re-layouts  27.6 us (3%)
  between operations  14.5 us (2%)
    reduce_scatter x1, waiting for transfers between devices, local(): lax.psum_scatter(grad_wgu, 'row', scatter_dimension=0, tiled=True)  96.2 us
    reduce_scatter x4, waiting for transfers between devices, column_sum(): lax.psum_scatter(product(left).astype(jnp.bfloat16), 'col', scatter_dimen...  88.2 us
    unnamed x16, waiting for transfers between devices  85.8 us
    reduce_scatter x1, waiting for transfers between devices, local(): lax.psum_scatter(grad_values_all, 'row', scatter_dimension=0, tiled=True)  76.9 us
    reduce_scatter x1, waiting for transfers between devices, local(): lax.psum_scatter(grad_down, 'row', scatter_dimension=1, tiled=True)  69.8 us
    reduce_scatter x1, waiting for transfers between devices, local(): lax.psum_scatter(grad_keys_all, 'row', scatter_dimension=0, tiled=True)  68 us
    all_gather x1, waiting for transfers between devices, local(): lax.all_gather(w_gate_up, 'row', axis=0, tiled=True)  43.2 us
    psum x1, blocking collectives, local(): lax.psum((grad_gain1, grad_bias1, grad_gain2, grad_bias2), ('row', 'col'))  40.1 us
  transfers between devices with their start and end apart: 14, of which 14 were waited for; matrix products, arithmetic and copies ran while one was open for 6% of the time, Pallas kernels for 0%

commit v1 on v0

--- a/solution.py
+++ b/solution.py
@@ -156,8 +156,9 @@
     )
     value_bf = mixed[:, 2].astype(jnp.bfloat16)
     run_max = jnp.full((local_heads, group), MASKED, jnp.float32)
-    key_piece = lax.all_gather(key_bf, "row", axis=0, tiled=True)
-    value_piece = lax.all_gather(value_bf, "row", axis=0, tiled=True)
+    x_next = jnp.concatenate([key_bf, value_bf], 1)
+    piece_out = jax.lax.all_gather(x_next, "row", axis=0, tiled=True)
+    key_piece, value_piece = jnp.split(piece_out, [key_bf.shape[1]], 1)
     count = key_piece.shape[0]
     seg_keys = seq_all
     scores, same = score_block(query_bf, seg_rows, key_piece, seg_keys, scale)

time: 919 us -> 996 us (1.084)
  waiting for transfers between devices: 598 us -> 670 us
    all_gather x2 -> x3, waiting for transfers between devices: 33 us -> 110 us  [the longest x1 46.3 us: local(): lax.all_gather(value_bf, 'row', axis=0, tiled=True)]
    unnamed x16 -> x17, waiting for transfers between devices: 85.8 us -> 86.3 us
  transfers between devices with their start and end apart: 14 -> 15, of which waited for: 14 -> 15; matrix products, arithmetic and copies ran while one was open for 6% -> 4% of each run, Pallas kernels for 0% -> 0%
where the time goes in v1:
time: 996 us; the launch traced here: 995 us
  waiting for transfers between devices  670 us (67%)
  blocking collectives  146 us (15%)
  matrix products  99.7 us (10%)
  other arithmetic  32.1 us (3%)
  local copies, waits for them, and re-layouts  30.9 us (3%)
  between operations  14.6 us (1%)
    reduce_scatter x1, waiting for transfers between devices, local(): lax.psum_scatter(grad_wgu, 'row', scatter_dimension=0, tiled=True)  96.1 us
    unnamed x17, waiting for transfers between devices  86.3 us
    reduce_scatter x4, waiting for transfers between devices, column_sum(): lax.psum_scatter(product(left).astype(jnp.bfloat16), 'col', scatter_dimen...  85.9 us
    reduce_scatter x1, waiting for transfers between devices, local(): lax.psum_scatter(grad_values_all, 'row', scatter_dimension=0, tiled=True)  76.6 us
    reduce_scatter x1, waiting for transfers between devices, local(): lax.psum_scatter(grad_down, 'row', scatter_dimension=1, tiled=True)  69.9 us
    reduce_scatter x1, waiting for transfers between devices, local(): lax.psum_scatter(grad_keys_all, 'row', scatter_dimension=0, tiled=True)  65.5 us
    all_gather x1, waiting for transfers between devices, local(): lax.all_gather(value_bf, 'row', axis=0, tiled=True)  46.3 us
    all_gather x1, waiting for transfers between devices, local(): lax.all_gather(w_gate_up, 'row', axis=0, tiled=True)  43.3 us
  transfers between devices with their start and end apart: 15, of which 15 were waited for; matrix products, arithmetic and copies ran while one was open for 4% of the time, Pallas kernels for 0%

profile of v1, /device:TPU:0, one launch (start us, length us, event | category | flops | bytes accessed | tf_op | source)
XLA Modules:
  0.0 994.7 jit_solution(7244871201534527878)
XLA Ops:
  8.3 38.8 %all_gather.34 = bf16[768,3,192]{2,1,0:T(4,128)(2,1)S(1)} all-gather(bf16[96,3,192]{2,1,0:T(4,128)(2,1)S(1)} %copy.45), channel_id=1, replica_groups=mesh['row'=8,'col'=4] {'row'}, dimensions={0}, use_global_device_ids=true | all-gather | bytes 995328 | tf_op jit(solution)/shard_map/all_gather | solution.py:134
  49.2 8.7 all_gather.33
  62.9 34.1 %all_gather.36 = bf16[192,768]{0,1:T(8,128)(2,1)} all-gather(bf16[192,96]{0,1:T(8,128)(2,1)S(1)} %copy.47), channel_id=1, replica_groups=mesh['row'=8,'col'=4] {'row'}, dimensions={1}, use_global_device_ids=true | all-gather | bytes 331776 | tf_op jit(solution)/shard_map/all_gather | solution.py:135
  98.3 27.8 %all-gather.7.cloned.1.call-done = bf16[4096,384]{0,1:T(8,128)(2,1)} async-done(((bf16[512,384]{0,1:T(8,128)(2,1)}), bf16[4096,384]{0,1:T(8,128)(2,1)}) %all-gather.7.cloned.1.call-update) | async-done | bytes 3145744 | tf_op jit(solution)/shard_map/all_gather | solution.py:160
  128.4 11.1 %select_reduce_fusion = (f32[3,512]{1,0:T(4,128)S(1)}, f32[3,512,4096]{2,1,0:T(8,128)}) fusion(pred[512,4096]{1,0:T(8,128)(4,1)S(1)} %broadcast_compare_fusion.1, bf16[4096,3,64]{0,2,1:T(8,128)(2,1)S(1)} %bitcast.174, bf16[512,3,32]{0,2,1:T(8,128)(2,1)S(1)} %copy-done.32, bf16[512,3,32]{0,2,1:T(8,128)(2,1)S(1)} %copy-done.30), kind=kOutput, calls=%fused_computation.16 | convolution fusion | flops 824572416 | bytes 29038592 | tf_op jit(solution)/shard_map/qhd,khd->hqk/dot_general | solution.py:87
  139.6 11.9 %fusion.8 = f32[3,512]{1,0:T(4,128)S(1)} fusion(f32[3,512,4096]{2,1,0:T(8,128)} %get-tuple-element.349, f32[3,512]{1,0:T(4,128)S(1)} %broadcast_maximum_fusion, pred[512,4096]{1,0:T(8,128)(4,1)S(1)} %broadcast_compare_fusion.1), kind=kLoop, calls=%fused_computation.17 | loop fusion | flops 25164288 | bytes 27275264 | tf_op jit(solution)/shard_map/reduce_sum | solution.py:167
  151.5 11.8 %fusion.29 = (bf16[512,3,64]{0,2,1:T(8,128)(2,1)S(1)}, f32[3,512,64]{1,2,0:T(8,128)}) fusion(f32[512,3]{0,1:T(4,128)S(1)} %bitcast.187, bf16[4096,3,64]{0,2,1:T(8,128)(2,1)S(1)} %bitcast.173, f32[3,512,4096]{2,1,0:T(8,128)} %get-tuple-element.349, f32[3,512]{1,0:T(4,128)S(1)} %broadcast_maximum_fusion, pred[512,4096]{1,0:T(8,128)(4,1)S(1)} %broadcast_compare_fusion.1), kind=kOutput, calls=%fused_computation.59 | convolution fusion | flops 830668800 | bytes 29437952 | tf_op jit(solution)/shard_map/hqk,khd->hqd/dot_general | solution.py:168
  167.8 19.2 %reduce-scatter.15.cloned.1.call-done = bf16[128,768]{1,0:T(8,128)(2,1)} async-done(((bf16[512,768]{1,0:T(8,128)(2,1)}), bf16[128,768]{1,0:T(8,128)(2,1)}) %reduce-scatter.15.cloned.1.call-update) | async-done | bytes 196624 | tf_op jit(solution)/shard_map/reduce_scatter | solution.py:77
  190.2 8.4 all_gather.37
  198.6 43.3 %all-gather.9.cloned.1.call-done = bf16[768,2,768]{2,0,1:T(8,128)(2,1)} async-done(((bf16[96,2,768]{2,0,1:T(8,128)(2,1)}), bf16[768,2,768]{2,0,1:T(8,128)(2,1)}) %all-gather.9.cloned.1.call-update) | async-done | bytes 2359312 | tf_op jit(solution)/shard_map/all_gather | solution.py:136
  247.1 36.7 %all-gather.11.cloned.1.call-done = bf16[768,768]{0,1:T(8,128)(2,1)} async-done(((bf16[768,96]{0,1:T(8,128)(2,1)}), bf16[768,768]{0,1:T(8,128)(2,1)}) %all-gather.11.cloned.1.call-update) | async-done | bytes 1179664 | tf_op jit(solution)/shard_map/all_gather | solution.py:137
  286.9 22.1 %reduce-scatter.17.cloned.1.call-done = bf16[128,768]{1,0:T(8,128)(2,1)} async-done(((bf16[512,768]{1,0:T(8,128)(2,1)}), bf16[128,768]{1,0:T(8,128)(2,1)}) %reduce-scatter.17.cloned.1.call-update) | async-done | bytes 196624 | tf_op jit(solution)/shard_map/reduce_scatter | solution.py:77
  327.7 21.3 %reduce-scatter.19.cloned.1.call-done = bf16[128,768]{1,0:T(8,128)(2,1)} async-done(((bf16[512,768]{1,0:T(8,128)(2,1)}), bf16[128,768]{1,0:T(8,128)(2,1)}) %reduce-scatter.19.cloned.1.call-update) | async-done | bytes 196624 | tf_op jit(solution)/shard_map/reduce_scatter | solution.py:77
  361.6 35.5 %all-gather.13.cloned.1.call-done = bf16[4096,192]{0,1:T(8,128)(2,1)} async-done(((bf16[512,192]{0,1:T(8,128)(2,1)}), bf16[4096,192]{0,1:T(8,128)(2,1)}) %all-gather.13.cloned.1.call-update) | async-done | bytes 1572880 | tf_op jit(solution)/shard_map/all_gather | solution.py:231
  397.1 46.3 %all-gather.15.cloned.1.call-done = bf16[4096,1,192]{0,2,1:T(8,128)(2,1)} async-done(((bf16[512,1,192]{0,2,1:T(8,128)(2,1)}), bf16[4096,1,192]{0,2,1:T(8,128)(2,1)}) %all-gather.15.cloned.1.call-update) | async-done | bytes 1572880 | tf_op jit(solution)/shard_map/all_gather | solution.py:232
  447.5 58.7 %while.18 = (s32[]{:T(128)}, f32[512,3,64]{0,2,1:T(8,128)S(1)}, f32[4096,192]{0,1:T(8,128)}, f32[4096,192]{0,1:T(8,128)}, bf16[4096,192]{0,1:T(8,128)(2,1)S(1)},...) while((s32[]{:T(128)}, f32[512,3,64]{0,2,1:T(8,128)S(1)}, ...), condition=%wide.region_18.19_spmd.clone, body=%wide.region_17.18_spmd.clone.sunk | while | flops 2045968384 | bytes 107786520 | solution.py:275
  513.6 65.5 %reduce-scatter.21.cloned.1.call-done = f32[512,192]{0,1:T(8,128)} async-done(((f32[4096,192]{0,1:T(8,128)}), f32[512,192]{0,1:T(8,128)}) %reduce-scatter.21.cloned.1.call-update) | async-done | bytes 393232 | tf_op jit(solution)/shard_map/reduce_scatter | solution.py:279
  580.4 76.6 %reduce-scatter.23.cloned.1.call-done = f32[512,192]{0,1:T(8,128)} async-done(((f32[4096,192]{0,1:T(8,128)}), f32[512,192]{0,1:T(8,128)}) %reduce-scatter.23.cloned.1.call-update) | async-done | bytes 393232 | tf_op jit(solution)/shard_map/reduce_scatter | solution.py:280
  666.9 40.0 %all-reduce = (f32[768]{0:T(1024)}, f32[768]{0:T(1024)}, f32[768]{0:T(1024)}, f32[768]{0:T(1024)}) all-reduce(f32[768]{0:T(1024)S(1)} %get-tuple-element.283, f32[768]{0:T(1024)S(1)} %get-tuple-element.288, f32[768]{0:T(1024)S(1)} %copy-done.41, f32[768]{0:T(1024)S(1)} %copy-done.42), channel_id=1, replica_groups=mesh['row'=8,'col'=4] {'row','col'}, use_global_device_ids=true, to_apply=%region_27.28 | all-reduce | flops 3072 | bytes 24576 | tf_op jit(solution)/shard_map/psum | solution.py:303
  706.9 15.6 %reduce-scatter.33.cloned.1.call-done = f32[96,192]{1,0:T(8,128)} async-done(((f32[768,192]{1,0:T(8,128)}), f32[96,192]{1,0:T(8,128)}) %reduce-scatter.33.cloned.1.call-update) | async-done | bytes 73744
  724.1 96.1 %reduce-scatter.27.cloned.1.call-done = f32[96,2,768]{2,0,1:T(8,128)} async-done(((f32[768,2,768]{2,0,1:T(8,128)}), f32[96,2,768]{2,0,1:T(8,128)}) %reduce-scatter.27.cloned.1.call-update) | async-done | bytes 589840 | tf_op jit(solution)/shard_map/reduce_scatter | solution.py:300
  822.5 23.3 %reduce-scatter.25.cloned.1.call-done = bf16[128,768]{1,0:T(8,128)(2,1)} async-done(((bf16[512,768]{1,0:T(8,128)(2,1)}), bf16[128,768]{1,0:T(8,128)(2,1)}) %reduce-scatter.25.cloned.1.call-update) | async-done | bytes 196624 | tf_op jit(solution)/shard_map/reduce_scatter | solution.py:77
  847.5 68.8 %reduce-scatter.31.cloned.1.call-done = f32[96,576]{1,0:T(8,128)} async-done(((f32[768,576]{1,0:T(8,128)}), f32[96,576]{1,0:T(8,128)}) %reduce-scatter.31.cloned.1.call-update) | async-done | bytes 221200
  918.3 69.9 %reduce-scatter.29.cloned.1.call-done = f32[768,96]{0,1:T(8,128)} async-done(((f32[768,768]{0,1:T(8,128)}), f32[768,96]{0,1:T(8,128)}) %reduce-scatter.29.cloned.1.call-update) | async-done | bytes 294928 | tf_op jit(solution)/shard_map/reduce_scatter | solution.py:301
  (224 shorter events, 147.0 us)
Async XLA Ops:
  7.2 119.0 %all-gather.7.cloned.1.call-start = ((), (), s32[]{:S(2)}) async-start(), calls=%async_computation.10 | async-start | bytes 3538944 | tf_op jit(solution)/shard_map/all_gather | solution.py:160
  62.6 124.3 %reduce-scatter.15.cloned.1.call-start = ((), (), s32[]{:S(2)}) async-start(), calls=%async_computation.11 | async-start | bytes 983040 | tf_op jit(solution)/shard_map/reduce_scatter | solution.py:77
  165.4 76.6 %all-gather.9.cloned.1.call-start = ((), (), s32[]{:S(2)}) async-start(), calls=%async_computation.12 | async-start | bytes 2654208 | tf_op jit(solution)/shard_map/all_gather | solution.py:136
  167.2 116.7 %all-gather.11.cloned.1.call-start = ((), (), s32[]{:S(2)}) async-start(), calls=%async_computation.13 | async-start | bytes 1327104 | tf_op jit(solution)/shard_map/all_gather | solution.py:137
  167.7 141.3 %reduce-scatter.17.cloned.1.call-start = ((), (), s32[]{:S(2)}) async-start(), calls=%async_computation.14 | async-start | bytes 983040 | tf_op jit(solution)/shard_map/reduce_scatter | solution.py:77
  247.1 64.3 %copy-start.7 = (bf16[512,768]{1,0:T(8,128)(2,1)}, bf16[512,768]{1,0:T(8,128)(2,1)S(1)}, u32[]{:S(2)}) copy-start(bf16[512,768]{1,0:T(8,128)(2,1)S(1)} %multiply_convert_fusion.2) | copy-start | bytes 2359300
  247.1 64.2 %copy-start.43 = (f32[768]{0:T(1024)S(1)}, f32[768]{0:T(1024)}, u32[]{:S(2)}) copy-start(f32[768]{0:T(1024)} %param.22) | copy-start | bytes 9220
  286.8 62.1 %reduce-scatter.19.cloned.1.call-start = ((), (), s32[]{:S(2)}) async-start(), calls=%async_computation.15 | async-start | bytes 983040 | tf_op jit(solution)/shard_map/reduce_scatter | solution.py:77
  325.1 72.0 %all-gather.13.cloned.1.call-start = ((), (), s32[]{:S(2)}) async-start(), calls=%async_computation.16 | async-start | bytes 1769472 | tf_op jit(solution)/shard_map/all_gather | solution.py:231
  325.9 117.5 %all-gather.15.cloned.1.call-start = ((), (), s32[]{:S(2)}) async-start(), calls=%async_computation.22 | async-start | bytes 1769472 | tf_op jit(solution)/shard_map/all_gather | solution.py:232
  326.7 252.5 %reduce-scatter.21.cloned.1.call-start = ((), (), s32[]{:S(2)}) async-start(), calls=%async_computation.17 | async-start | bytes 3538944 | tf_op jit(solution)/shard_map/reduce_scatter | solution.py:279
  506.3 150.8 %reduce-scatter.23.cloned.1.call-start = ((), (), s32[]{:S(2)}) async-start(), calls=%async_computation.18 | async-start | bytes 3538944 | tf_op jit(solution)/shard_map/reduce_scatter | solution.py:280
  506.8 215.6 %reduce-scatter.33.cloned.1.call-start = ((), (), s32[]{:S(2)}) async-start(), calls=%async_computation.24 | async-start | bytes 884736
  508.8 311.4 %reduce-scatter.27.cloned.1.call-start = ((), (), s32[]{:S(2)}) async-start(), calls=%async_computation.20 | async-start | bytes 5308416 | tf_op jit(solution)/shard_map/reduce_scatter | solution.py:300
  513.5 66.7 %copy-start.26 = (f32[512,32]{0,1:T(8,128)S(1)}, f32[512,32]{0,1:T(8,128)}, u32[]{:S(2)}) copy-start(f32[512,32]{0,1:T(8,128)} %copy-done.25) | copy-start | bytes 196612
  513.5 66.7 %copy-start.28 = (f32[512,32]{0,1:T(8,128)S(1)}, f32[512,32]{0,1:T(8,128)}, u32[]{:S(2)}) copy-start(f32[512,32]{0,1:T(8,128)} %copy-done.27) | copy-start | bytes 196612
  513.5 145.2 %copy-start.9 = (bf16[768,3,192]{0,2,1:T(8,128)(2,1)S(1)}, bf16[768,3,192]{0,2,1:T(8,128)(2,1)}, u32[]{:S(2)}) copy-start(bf16[768,3,192]{0,2,1:T(8,128)(2,1)} %copy.46) | copy-start | bytes 2654212
  513.6 332.3 %reduce-scatter.25.cloned.1.call-start = ((), (), s32[]{:S(2)}) async-start(), calls=%async_computation.19 | async-start | bytes 983040 | tf_op jit(solution)/shard_map/reduce_scatter | solution.py:77
  580.4 80.2 %copy-start.33 = (bf16[512,3,64]{0,2,1:T(8,128)(2,1)}, bf16[512,3,64]{0,2,1:T(8,128)(2,1)S(1)}, u32[]{:S(2)}) copy-start(bf16[512,3,64]{0,2,1:T(8,128)(2,1)S(1)} %pad_maximum_fusion.9) | copy-start | bytes 589828
  580.4 80.4 %copy-start.15 = (bf16[512,768]{1,0:T(8,128)(2,1)S(1)}, bf16[512,768]{1,0:T(8,128)(2,1)}, u32[]{:S(2)}) copy-start(bf16[512,768]{1,0:T(8,128)(2,1)} %copy-done.14) | copy-start | bytes 2359300
  580.4 80.1 %copy-start.34 = (bf16[512,3,64]{0,2,1:T(8,128)(2,1)}, bf16[512,3,64]{0,2,1:T(8,128)(2,1)S(1)}, u32[]{:S(2)}) copy-start(bf16[512,3,64]{0,2,1:T(8,128)(2,1)S(1)} %pad_maximum_fusion.10) | copy-start | bytes 589828
  660.6 255.7 %reduce-scatter.31.cloned.1.call-start = ((), (), s32[]{:S(2)}) async-start(), calls=%async_computation.23 | async-start | bytes 2211840
  664.4 323.7 %reduce-scatter.29.cloned.1.call-start = ((), (), s32[]{:S(2)}) async-start(), calls=%async_computation.21 | async-start | bytes 2654208 | tf_op jit(solution)/shard_map/reduce_scatter | solution.py:301
  666.8 179.0 %copy-start.19 = (f32[128,768]{1,0:T(8,128)S(1)}, f32[128,768]{1,0:T(8,128)}, u32[]{:S(2)}) copy-start(f32[128,768]{1,0:T(8,128)} %get-tuple-element.320) | copy-start | bytes 1179652
  (43 other events, 524.7 us)
Sparse Core Ops, SparseCore 0:
  62.8 63.3 all-gather.6
  165.5 21.4 reduce-scatter.14
  190.0 51.9 all-gather.8
  244.2 39.5 all-gather.10
  286.9 22.0 reduce-scatter.16
  325.2 23.6 reduce-scatter.18
  351.7 45.3 all-gather.12
  399.9 43.4 all-gather.14
  506.4 72.7 reduce-scatter.20
  583.1 73.9 reduce-scatter.22
  660.7 61.6 reduce-scatter.32
  726.0 94.1 reduce-scatter.26
  822.7 23.0 reduce-scatter.24
  849.6 66.7 reduce-scatter.30
  920.2 67.9 reduce-scatter.28
